TPU v7x, 32 devices: a whole 2x2x4 slice. The times are simulated.
32 devices in a mesh: seq: 16 (over z, x, core), tp: 2 (over y).
Axes of the slice: x: 2, y: 2, z: 4, core: 2. Of those that a mesh axis runs over, the one named last changes fastest.
Arguments:
- normed_input: bfloat16 [2048, 4096], P(('seq', 'tp')), may hold values from -6 to 6
- output_gradient: bfloat16 [2048, 14336], P('seq', 'tp'), may hold values from -0.75 to 0.75
- adapter_down: bfloat16 [64, 16, 4096], P('seq', None, 'tp'), may hold values from -0.09375 to 0.09375
- adapter_up: bfloat16 [64, 16, 14336], P('seq', None, 'tp'), may hold values from -1.5 to 1.5
- adapter_of_block: int32 [16], P('seq'), may hold values from 0 to 63
- live_per_block: int32 [16], P('seq'), may hold values from 32 to 128, as said below
- adapter_home_row: int32 [64], replicated, may hold values from 0 to 63, each once
Outputs:
- adapter_output: bfloat16 [2048, 14336], P('seq', 'tp')
- input_gradient: bfloat16 [2048, 4096], P(('seq', 'tp'))
- down_gradient: float32 [64, 16, 4096], P('seq', None, 'tp')
- up_gradient: float32 [64, 16, 14336], P('seq', None, 'tp')
Inputs may be any that keep to these rules, and one draw needn't show every extreme that they name: `live_per_block`: every eighth block, counting from block 0, is full. `adapter_home_row`: each row appears once.
All inputs are finite; a program needn't handle non-finite values.
Results may differ from a plain program's by a relative error of at most 0.0051.
Values may be sent and summed in bfloat16 or wider, within the bound.
A program may use at most 128 MiB of HBM per device.

v0:
```python
import jax
import jax.numpy as jnp
from jax import lax
from jax.sharding import PartitionSpec as P

adapter_scale = 2.0


def per_device(
    normed_input,
    output_gradient,
    adapter_down,
    adapter_up,
    adapter_of_block,
    live_per_block,
    adapter_home_row,
):
    seq_count = lax.axis_size("seq")
    total_blocks = adapter_of_block.shape[0]
    token_rows = output_gradient.shape[0]
    block_length = token_rows // total_blocks
    adapters = adapter_home_row.shape[0]
    rank_projected = adapter_down.shape[1]
    width_slice = adapter_down.shape[2]
    hidden_slice = adapter_up.shape[2]
    all_a, all_b = (
        lax.all_gather(adapter_down, "seq", axis=0, tiled=True),
        lax.all_gather(adapter_up, "seq", axis=0, tiled=True),
    )
    chosen = (adapter_of_block[:, None] == jnp.arange(adapters, dtype=jnp.int32)[None, :]).astype(
        jnp.float32
    )
    chosen_low = chosen.astype(jnp.bfloat16)
    pick_a = jnp.einsum(
        "ba,ard->brd", chosen_low, all_a, preferred_element_type=jnp.float32
    ).astype(jnp.bfloat16)
    pick_b = jnp.einsum(
        "ba,arf->brf", chosen_low, all_b, preferred_element_type=jnp.float32
    ).astype(jnp.bfloat16)
    token_live_mask = (
        jnp.arange(block_length, dtype=jnp.int32)[None, :] < live_per_block[:, None]
    ).astype(jnp.float32)[:, :, None]
    g_blocks = output_gradient.reshape(total_blocks, block_length, hidden_slice)
    back_part = jnp.einsum("btf,brf->btr", g_blocks, pick_b, preferred_element_type=jnp.float32)
    back_part = back_part.reshape(total_blocks, block_length * rank_projected)
    x_tensor = lax.all_to_all(normed_input, "tp", split_axis=1, concat_axis=0, tiled=True)
    x_blocks = x_tensor.reshape(total_blocks, block_length, width_slice)
    down_part = jnp.einsum("btd,brd->btr", x_blocks, pick_a, preferred_element_type=jnp.float32)
    down_part = down_part.reshape(total_blocks, block_length * rank_projected)
    down_sum, backward_total = lax.psum((down_part, back_part), "tp")
    down_reduced = (
        down_sum.reshape(total_blocks, block_length, rank_projected) * token_live_mask
    ).astype(jnp.bfloat16)
    backward_reduced = (
        adapter_scale
        * backward_total.reshape(total_blocks, block_length, rank_projected)
        * token_live_mask
    ).astype(jnp.bfloat16)
    grad_tensor = jnp.einsum(
        "btr,brd->btd", backward_reduced, pick_a, preferred_element_type=jnp.float32
    )
    grad_tensor = grad_tensor.astype(jnp.bfloat16).reshape(token_rows, width_slice)
    input_gradient = lax.all_to_all(grad_tensor, "tp", split_axis=0, concat_axis=1, tiled=True)
    grad_a_blocks = jnp.einsum(
        "btr,btd->brd", backward_reduced, x_blocks, preferred_element_type=jnp.float32
    )
    adapter_output = adapter_scale * jnp.einsum(
        "btr,brf->btf", down_reduced, pick_b, preferred_element_type=jnp.float32
    )
    adapter_output = adapter_output.astype(jnp.bfloat16).reshape(token_rows, hidden_slice)
    up_gradient_blocks = adapter_scale * jnp.einsum(
        "btr,btf->brf", down_reduced, g_blocks, preferred_element_type=jnp.float32
    )
    block_row = jnp.dot(
        chosen, adapter_home_row.astype(jnp.float32), precision=lax.Precision.HIGHEST
    )
    slots_each = adapters // seq_count
    my_rows = (lax.axis_index("seq") * slots_each + jnp.arange(slots_each, dtype=jnp.int32)).astype(
        jnp.float32
    )
    piece_a = lax.all_gather(grad_a_blocks, "seq", axis=0, tiled=True)
    piece_b = lax.all_gather(up_gradient_blocks, "seq", axis=0, tiled=True)
    piece_rows = lax.all_gather(block_row, "seq", axis=0, tiled=True)
    match = (piece_rows[:, None] == my_rows[None, :]).astype(jnp.float32)
    following_down = jnp.einsum("ns,nrd->srd", match, piece_a, precision=lax.Precision.HIGHEST)
    following_up = jnp.einsum("ns,nrf->srf", match, piece_b, precision=lax.Precision.HIGHEST)
    return (adapter_output, input_gradient, following_down, following_up)


def solution(mesh):
    placed = (
        P(("seq", "tp"), None),
        P("seq", "tp"),
        P("seq", None, "tp"),
        P("seq", None, "tp"),
        P("seq"),
        P("seq"),
        P(),
    )
    return jax.shard_map(
        per_device,
        mesh=mesh,
        in_specs=placed,
        out_specs=(
            P("seq", "tp"),
            P(("seq", "tp"), None),
            P("seq", None, "tp"),
            P("seq", None, "tp"),
        ),
        check_vma=False,
    )
```

profile of v0, /device:TPU:0, one launch (start us, length us, event | category | flops | bytes accessed | tf_op | source)
XLA Modules:
  0.0 334.9 jit_solution(5447570768813441117)
XLA Ops:
  7.2 0.7 all-gather.7.cloned.1.call-update
  8.0 0.7 all-gather.9.cloned.1.call-update
  8.7 1.9 copy.62
  10.5 4.3 %all-to-all-start = ((bf16[64,2,2048]{2,0,1:T(8,128)(2,1)}), bf16[64,2,2048]{2,0,1:T(8,128)(2,1)S(1)}, u32[]{:S(2)}, u32[]{:S(2)}) async-start(bf16[64,2,2048]{2,0,1:T(8,128)(2,1)} %bitcast.50), calls=%async_computation | async-start | bytes 1048576 | tf_op jit(solution)/shard_map/all_to_all | solution.py:46
  16.4 0.1 mul.58
  16.5 46.8 %all-gather.7.cloned.1.call-done = bf16[64,16,2048]{2,1,0:T(8,128)(2,1)} async-done(((bf16[4,16,2048]{2,1,0:T(8,128)(2,1)}), bf16[64,16,2048]{2,1,0:T(8,128)(2,1)}) %all-gather.7.cloned.1.call-update) | async-done | bytes 4194320 | tf_op jit(solution)/shard_map/all_gather | solution.py:27
  63.3 6.7 %fusion.5 = bf16[1,16,2048]{2,0,1:T(2,128)(2,1)S(1)} fusion(bf16[64,16,2048]{2,1,0:T(8,128)(2,1)} %all-gather.7.cloned.1.call-done, s32[]{:T(128)} %bitcast.51), kind=kOutput, calls=%fused_computation.7 | convolution fusion | flops 4194496 | bytes 4259844 | tf_op jit(solution)/shard_map/ba,ard->brd/dot_general | solution.py:34
  70.0 0.2 convolution_bitcast_fusion.1
  70.2 0.1 copy.32
  70.3 0.1 reshape.142
  70.4 107.1 %all-gather.9.cloned.1.call-done = bf16[64,16,7168]{2,1,0:T(8,128)(2,1)} async-done(((bf16[4,16,7168]{2,1,0:T(8,128)(2,1)}), bf16[64,16,7168]{2,1,0:T(8,128)(2,1)}) %all-gather.9.cloned.1.call-update) | async-done | bytes 14680080 | tf_op jit(solution)/shard_map/all_gather | solution.py:28
  177.5 20.9 %fusion = bf16[1,16,7168]{2,0,1:T(2,128)(2,1)S(1)} fusion(bf16[64,16,7168]{2,1,0:T(8,128)(2,1)} %all-gather.9.cloned.1.call-done, s32[]{:T(128)} %bitcast.52), kind=kOutput, calls=%fused_computation | convolution fusion | flops 14680256 | bytes 14909444 | tf_op jit(solution)/shard_map/ba,arf->brf/dot_general | solution.py:37
  198.4 0.6 convolution_bitcast_fusion
  199.0 0.1 copy.33
  199.1 0.1 reshape.143
  199.2 8.1 %all-reduce.1 = (f32[1,2048]{1,0:T(1,128)S(1)}, f32[1,2048]{1,0:T(1,128)S(1)}) all-reduce(f32[1,2048]{1,0:T(1,128)S(1)} %reshape.142, f32[1,2048]{1,0:T(1,128)S(1)} %reshape.143), channel_id=1, replica_groups=mesh['seq'=16,'tp'=2] {'tp'}, use_global_device_ids=true, to_apply=%region_0.0 | all-reduce | flops 4096 | bytes 32768 | tf_op jit(solution)/shard_map/psum | solution.py:50
  207.4 0.9 fusion.24
  208.4 1.2 convolution_multiply_fusion.1
  209.7 0.6 dynamic-slice
  210.2 0.6 fusion.19
  210.8 1.4 dynamic-update-slice
  212.2 30.0 %all-reduce = f32[16]{0:T(128)S(1)} all-reduce(f32[16]{0:T(128)S(1)} %dynamic-update-slice), channel_id=1, replica_groups=mesh['seq'=16,'tp'=2] {'seq'}, use_global_device_ids=true, to_apply=%add | all-reduce | flops 16 | bytes 128
  242.2 1.1 convolution_convert_fusion
  243.3 3.7 %all-to-all-start.1 = ((bf16[2,64,2048]{2,1,0:T(8,128)(2,1)}), bf16[2,64,2048]{2,1,0:T(8,128)(2,1)S(1)}, u32[]{:S(2)}, u32[]{:S(2)}) async-start(bf16[2,64,2048]{2,1,0:T(8,128)(2,1)} %bitcast.10), calls=%async_computation.1 | async-start | bytes 1048576 | tf_op jit(solution)/shard_map/all_to_all | solution.py:63
  247.0 1.8 fusion.2
  248.9 6.0 %all-to-all-done.1 = bf16[2,64,2048]{2,1,0:T(8,128)(2,1)S(1)} async-done(((bf16[2,64,2048]{2,1,0:T(8,128)(2,1)}), bf16[2,64,2048]{2,1,0:T(8,128)(2,1)S(1)}, u32[]{:S(2)}, u32[]{:S(2)}) %all-to-all-start.1) | async-done | bytes 524320 | tf_op jit(solution)/shard_map/all_to_all | solution.py:63
  254.9 0.8 copy.46
  255.7 3.6 %fusion.7 = f32[4,16,2048]{2,0,1:T(4,128)S(1)} fusion(f32[16,16,2048]{2,1,0:T(8,128)} %bitcast.59, f32[16]{0:T(128)S(1)} %all-reduce, f32[4]{0:T(128)S(1)} %add_convert_fusion), kind=kOutput, calls=%fused_computation.10 | convolution fusion | flops 25165888 | bytes 2621520 | tf_op jit(solution)/shard_map/ns,nrd->srd/dot_general | solution.py:85
  259.3 1.1 copy.37
  260.4 56.1 %all-gather.13.cloned.1.call-done = f32[256,7168]{1,0:T(8,128)} async-done(((f32[16,7168]{1,0:T(8,128)}), f32[256,7168]{1,0:T(8,128)}) %all-gather.13.cloned.1.call-update) | async-done | bytes 7340048 | tf_op jit(solution)/shard_map/all_gather | solution.py:82
  316.5 9.5 %fusion.3 = f32[4,16,7168]{2,0,1:T(4,128)S(1)} fusion(f32[16,16,7168]{2,1,0:T(8,128)} %bitcast.56, f32[16]{0:T(128)S(1)} %all-reduce, f32[4]{0:T(128)S(1)} %add_convert_fusion), kind=kOutput, calls=%fused_computation.5 | convolution fusion | flops 88080448 | bytes 9175120 | tf_op jit(solution)/shard_map/ns,nrf->srf/dot_general | solution.py:86
  326.1 2.3 copy.38
  (24 shorter events, 0.7 us)
Async XLA Ops:
  7.2 191.2 %copy-start = (bf16[128,7168]{1,0:T(8,128)(2,1)S(1)}, bf16[128,7168]{1,0:T(8,128)(2,1)}, u32[]{:S(2)}) copy-start(bf16[128,7168]{1,0:T(8,128)(2,1)} %param.8) | copy-start | bytes 5505028
  7.2 56.1 %all-gather.7.cloned.1.call-start = ((), (), s32[]{:S(2)}) async-start(), calls=%async_computation.2 | async-start | bytes 4456448 | tf_op jit(solution)/shard_map/all_gather | solution.py:27
  7.9 169.6 %all-gather.9.cloned.1.call-start = ((), (), s32[]{:S(2)}) async-start(), calls=%async_computation.3 | async-start | bytes 15597568 | tf_op jit(solution)/shard_map/all_gather | solution.py:28
  10.5 59.4 %all-to-all-start = ((bf16[64,2,2048]{2,0,1:T(8,128)(2,1)}), bf16[64,2,2048]{2,0,1:T(8,128)(2,1)S(1)}, u32[]{:S(2)}, u32[]{:S(2)}) async-start(bf16[64,2,2048]{2,0,1:T(8,128)(2,1)} %bitcast.50), calls=%async_computation | async-start | bytes 1048576 | tf_op jit(solution)/shard_map/all_to_all | solution.py:46
  14.8 240.9 %all-gather.11.cloned.1.call-start = ((), (), s32[]{:S(2)}) async-start(), calls=%async_computation.4 | async-start | bytes 2228224 | tf_op jit(solution)/shard_map/all_gather | solution.py:81
  198.4 11.3 %copy-start.2 = (u32[32]{0:T(128)S(1)}, u32[32]{0:T(128)}, u32[]{:S(2)}) copy-start(u32[32]{0:T(128)} %constant.20) | copy-start | bytes 388
  198.4 11.9 %copy-start.1 = (s32[64]{0:T(128)S(1)}, s32[64]{0:T(128)}, u32[]{:S(2)}) copy-start(s32[64]{0:T(128)} %param.13) | copy-start | bytes 772
  208.3 108.2 %all-gather.13.cloned.1.call-start = ((), (), s32[]{:S(2)}) async-start(), calls=%async_computation.5 | async-start | bytes 7798784 | tf_op jit(solution)/shard_map/all_gather | solution.py:82
  243.3 11.6 %all-to-all-start.1 = ((bf16[2,64,2048]{2,1,0:T(8,128)(2,1)}), bf16[2,64,2048]{2,1,0:T(8,128)(2,1)S(1)}, u32[]{:S(2)}, u32[]{:S(2)}) async-start(bf16[2,64,2048]{2,1,0:T(8,128)(2,1)} %bitcast.10), calls=%async_computation.1 | async-start | bytes 1048576 | tf_op jit(solution)/shard_map/all_to_all | solution.py:63
Sparse Core Ops, SparseCore 0:
  10.1 53.0 all-gather.6
  65.6 111.8 all-gather.8
  208.4 38.7 all-gather.10
  249.9 66.5 all-gather.12
where the time goes:
time: 335 us
  waiting for transfers between devices  217 us (65%)
  matrix products  46.5 us (14%)
  blocking collectives  38 us (11%)
  between operations  15.2 us (5%)
  local copies, waits for them, and re-layouts  9.04 us (3%)
  starting transfers between devices  8.09 us (2%)
    all_gather x1, waiting for transfers between devices, per_device(): lax.all_gather(adapter_up, 'seq', axis=0, tiled=True)  107 us
    all_gather x1, waiting for transfers between devices, per_device(): piece_b = lax.all_gather(up_gradient_blocks, 'seq', axis=0, tiled=True)  56.1 us
    all_gather x1, waiting for transfers between devices, per_device(): lax.all_gather(adapter_down, 'seq', axis=0, tiled=True)  46.8 us
    unnamed x1, blocking collectives  30 us
    dot_general x1, matrix products, per_device(): jnp.einsum('ba,arf->brf', chosen_low, all_b, preferred_element_type=jnp.f...  20.9 us
    dot_general x1, matrix products, per_device(): jnp.einsum('ns,nrf->srf', match, piece_b, precision=lax.Precision.HIGHEST)  9.53 us
    psum x1, blocking collectives, per_device(): down_sum, backward_total = lax.psum((down_part, back_part), 'tp')  8.06 us
    dot_general x1, matrix products, per_device(): jnp.einsum('ba,ard->brd', chosen_low, all_a, preferred_element_type=jnp.f...  6.7 us
  transfers between devices with their start and end apart: 6, of which 4 were waited for; matrix products, arithmetic and copies ran while one was open for 6% of the time, Pallas kernels for 0%

commit v1 on v0

--- a/solution.py
+++ b/solution.py
@@ -79,11 +79,28 @@
         jnp.float32
     )
     piece_a = lax.all_gather(grad_a_blocks, "seq", axis=0, tiled=True)
-    piece_b = lax.all_gather(up_gradient_blocks, "seq", axis=0, tiled=True)
     piece_rows = lax.all_gather(block_row, "seq", axis=0, tiled=True)
     match = (piece_rows[:, None] == my_rows[None, :]).astype(jnp.float32)
     following_down = jnp.einsum("ns,nrd->srd", match, piece_a, precision=lax.Precision.HIGHEST)
-    following_up = jnp.einsum("ns,nrf->srf", match, piece_b, precision=lax.Precision.HIGHEST)
+    count, index = (lax.axis_size("seq"), lax.axis_index("seq"))
+    left = [(i, (i - 1) % count) for i in range(count)]
+    rows = up_gradient_blocks.shape[0]
+    held = up_gradient_blocks
+    so_far = jnp.einsum(
+        "ns,nrf->srf",
+        lax.dynamic_slice_in_dim(match, index * rows, held.shape[0], axis=0),
+        held,
+        precision=lax.Precision.HIGHEST,
+    )
+    for step in range(1, count):
+        held = lax.ppermute(held, "seq", left)
+        so_far = so_far + jnp.einsum(
+            "ns,nrf->srf",
+            lax.dynamic_slice_in_dim(match, (index + step) % count * rows, held.shape[0], axis=0),
+            held,
+            precision=lax.Precision.HIGHEST,
+        )
+    following_up = so_far
     return (adapter_output, input_gradient, following_down, following_up)
 
 

time: 335 us -> 414 us (1.24)
  starting transfers between devices: 8.09 us -> 67.9 us
  waiting for transfers between devices: 217 us -> 236 us
  matrix products: 46.5 us -> 36.3 us
  other arithmetic: 0.67 us -> 6.09 us
  local copies, waits for them, and re-layouts: 9.04 us -> 13.3 us
    ppermute x0 -> x15, waiting for transfers between devices: none -> 79.6 us  [per_device(): held = lax.ppermute(held, 'seq', left)]
    ppermute x0 -> x15, starting transfers between devices: none -> 60.1 us  [per_device(): held = lax.ppermute(held, 'seq', left)]
    all_gather x1 -> x0, waiting for transfers between devices: 56.1 us -> none  [per_device(): piece_b = lax.all_gather(up_gradient_blocks, 'seq', axis=0, tiled=True)]
    dot_general x1 -> x0, matrix products: 9.53 us -> none  [per_device(): jnp.einsum('ns,nrf->srf', match, piece_b, precision=lax.Precision.HIGHEST)]
    add x0 -> x1, other arithmetic: none -> 5.26 us  [per_device(): so_far + jnp.einsum('ns,nrf->srf', lax.dynamic_slice_in_dim(match, (index...]
    all_to_all x1, waiting for transfers between devices: 6 us -> 1.03 us  [per_device(): lax.all_to_all(grad_tensor, 'tp', split_axis=0, concat_axis=1, tiled=True)]
    unnamed x11 -> x46, local copies, waits for them, and re-layouts: 5.4 us -> 9.65 us
  transfers between devices with their start and end apart: 6 -> 20, of which waited for: 4 -> 16; matrix products, arithmetic and copies ran while one was open for 6% -> 5% of each run, Pallas kernels for 0% -> 0%
where the time goes in v1:
time: 414 us; the launch traced here: 413 us
  waiting for transfers between devices  236 us (57%)
  starting transfers between devices  67.9 us (16%)
  blocking collectives  38.4 us (9%)
  matrix products  36.3 us (9%)
  between operations  15.4 us (4%)
  local copies, waits for them, and re-layouts  13.3 us (3%)
  other arithmetic  6.09 us (1%)
    all_gather x1, waiting for transfers between devices, per_device(): lax.all_gather(adapter_up, 'seq', axis=0, tiled=True)  107 us
    ppermute x15, waiting for transfers between devices, per_device(): held = lax.ppermute(held, 'seq', left)  79.6 us
    ppermute x15, starting transfers between devices, per_device(): held = lax.ppermute(held, 'seq', left)  60.1 us
    all_gather x1, waiting for transfers between devices, per_device(): lax.all_gather(adapter_down, 'seq', axis=0, tiled=True)  46.8 us
    unnamed x1, blocking collectives  30.4 us
    dot_general x1, matrix products, per_device(): jnp.einsum('ba,arf->brf', chosen_low, all_b, preferred_element_type=jnp.f...  20.9 us
    unnamed x46, local copies, waits for them, and re-layouts  9.65 us
  transfers between devices with their start and end apart: 20, of which 16 were waited for; matrix products, arithmetic and copies ran while one was open for 5% of the time, Pallas kernels for 0%

profile of v1, /device:TPU:0, one launch (start us, length us, event | category | flops | bytes accessed | tf_op | source)
XLA Modules:
  0.0 413.3 jit_solution(5628434406198278248)
XLA Ops:
  16.5 46.8 %all-gather.5.cloned.1.call-done = bf16[64,16,2048]{2,1,0:T(8,128)(2,1)} async-done(((bf16[4,16,2048]{2,1,0:T(8,128)(2,1)}), bf16[64,16,2048]{2,1,0:T(8,128)(2,1)}) %all-gather.5.cloned.1.call-update) | async-done | bytes 4194320 | tf_op jit(solution)/shard_map/all_gather | solution.py:27
  63.3 6.7 %fusion.3 = bf16[1,16,2048]{2,0,1:T(2,128)(2,1)S(1)} fusion(bf16[64,16,2048]{2,1,0:T(8,128)(2,1)} %all-gather.5.cloned.1.call-done, s32[]{:T(128)} %bitcast.96), kind=kOutput, calls=%fused_computation.5 | convolution fusion | flops 4194496 | bytes 4259844 | tf_op jit(solution)/shard_map/ba,ard->brd/dot_general | solution.py:34
  70.4 107.1 %all-gather.7.cloned.1.call-done = bf16[64,16,7168]{2,1,0:T(8,128)(2,1)} async-done(((bf16[4,16,7168]{2,1,0:T(8,128)(2,1)}), bf16[64,16,7168]{2,1,0:T(8,128)(2,1)}) %all-gather.7.cloned.1.call-update) | async-done | bytes 14680080 | tf_op jit(solution)/shard_map/all_gather | solution.py:28
  177.5 20.9 %fusion = bf16[1,16,7168]{2,0,1:T(2,128)(2,1)S(1)} fusion(bf16[64,16,7168]{2,1,0:T(8,128)(2,1)} %all-gather.7.cloned.1.call-done, s32[]{:T(128)} %bitcast.97), kind=kOutput, calls=%fused_computation | convolution fusion | flops 14680256 | bytes 14909444 | tf_op jit(solution)/shard_map/ba,arf->brf/dot_general | solution.py:37
  199.2 8.1 %all-reduce.1 = (f32[1,2048]{1,0:T(1,128)S(1)}, f32[1,2048]{1,0:T(1,128)S(1)}) all-reduce(f32[1,2048]{1,0:T(1,128)S(1)} %reshape.269, f32[1,2048]{1,0:T(1,128)S(1)} %reshape.270), channel_id=1, replica_groups=mesh['seq'=16,'tp'=2] {'tp'}, use_global_device_ids=true, to_apply=%region_0.0 | all-reduce | flops 4096 | bytes 32768 | tf_op jit(solution)/shard_map/psum | solution.py:50
  207.8 6.0 %collective-permute-done = f32[1,16,7168]{2,1,0:T(8,128)S(1)} collective-permute-done((f32[1,16,7168]{2,1,0:T(8,128)S(1)}, f32[1,16,7168]{2,1,0:T(8,128)S(1)}, u32[]{:S(2)}, u32[]{:S(2)}) %collective-permute-start) | collective-permute-done | bytes 458784 | tf_op jit(solution)/shard_map/ppermute | solution.py:96
  214.6 4.6 %collective-permute-start.1 = (f32[1,16,7168]{2,1,0:T(8,128)S(1)}, f32[1,16,7168]{2,1,0:T(8,128)S(1)}, u32[]{:S(2)}, u32[]{:S(2)}) collective-permute-start(f32[1,16,7168]{2,1,0:T(8,128)S(1)} %collective-permute-done), channel_id=1, source_target_pairs={{0,30},{2,0},{4,2},{6,4},{8,6},{10,8},{12,10},{14,12},{16,14},{18,... | collective-permute-start | bytes 1376264 | tf_op jit(solution)/shard_map/ppermute | solution.py:96
  219.2 6.0 %collective-permute-done.1 = f32[1,16,7168]{2,1,0:T(8,128)S(1)} collective-permute-done((f32[1,16,7168]{2,1,0:T(8,128)S(1)}, f32[1,16,7168]{2,1,0:T(8,128)S(1)}, u32[]{:S(2)}, u32[]{:S(2)}) %collective-permute-start.1) | collective-permute-done | bytes 458784 | tf_op jit(solution)/shard_map/ppermute | solution.py:96
  226.0 4.6 %collective-permute-start.2 = (f32[1,16,7168]{2,1,0:T(8,128)S(1)}, f32[1,16,7168]{2,1,0:T(8,128)S(1)}, u32[]{:S(2)}, u32[]{:S(2)}) collective-permute-start(f32[1,16,7168]{2,1,0:T(8,128)S(1)} %collective-permute-done.1), channel_id=1, source_target_pairs={{0,30},{2,0},{4,2},{6,4},{8,6},{10,8},{12,10},{14,12},{16,14},{18,... | collective-permute-start | bytes 1376264 | tf_op jit(solution)/shard_map/ppermute | solution.py:96
  230.6 6.0 %collective-permute-done.2 = f32[1,16,7168]{2,1,0:T(8,128)S(1)} collective-permute-done((f32[1,16,7168]{2,1,0:T(8,128)S(1)}, f32[1,16,7168]{2,1,0:T(8,128)S(1)}, u32[]{:S(2)}, u32[]{:S(2)}) %collective-permute-start.2) | collective-permute-done | bytes 458784 | tf_op jit(solution)/shard_map/ppermute | solution.py:96
  237.4 4.6 %collective-permute-start.3 = (f32[1,16,7168]{2,1,0:T(8,128)S(1)}, f32[1,16,7168]{2,1,0:T(8,128)S(1)}, u32[]{:S(2)}, u32[]{:S(2)}) collective-permute-start(f32[1,16,7168]{2,1,0:T(8,128)S(1)} %collective-permute-done.2), channel_id=1, source_target_pairs={{0,30},{2,0},{4,2},{6,4},{8,6},{10,8},{12,10},{14,12},{16,14},{18,... | collective-permute-start | bytes 1376264 | tf_op jit(solution)/shard_map/ppermute | solution.py:96
  242.0 6.0 %collective-permute-done.3 = f32[1,16,7168]{2,1,0:T(8,128)S(1)} collective-permute-done((f32[1,16,7168]{2,1,0:T(8,128)S(1)}, f32[1,16,7168]{2,1,0:T(8,128)S(1)}, u32[]{:S(2)}, u32[]{:S(2)}) %collective-permute-start.3) | collective-permute-done | bytes 458784 | tf_op jit(solution)/shard_map/ppermute | solution.py:96
  248.7 4.6 %collective-permute-start.4 = (f32[1,16,7168]{2,1,0:T(8,128)S(1)}, f32[1,16,7168]{2,1,0:T(8,128)}, u32[]{:S(2)}, u32[]{:S(2)}) collective-permute-start(f32[1,16,7168]{2,1,0:T(8,128)S(1)} %collective-permute-done.3), channel_id=1, source_target_pairs={{0,30},{2,0},{4,2},{6,4},{8,6},{10,8},{12,10},{14,12},{16,14},{18,... | collective-permute-start | bytes 1376264 | tf_op jit(solution)/shard_map/ppermute | solution.py:96
  253.3 6.0 %collective-permute-done.4 = f32[1,16,7168]{2,1,0:T(8,128)} collective-permute-done((f32[1,16,7168]{2,1,0:T(8,128)S(1)}, f32[1,16,7168]{2,1,0:T(8,128)}, u32[]{:S(2)}, u32[]{:S(2)}) %collective-permute-start.4) | collective-permute-done | bytes 458784 | tf_op jit(solution)/shard_map/ppermute | solution.py:96
  259.3 4.7 %collective-permute-start.5 = (f32[1,16,7168]{2,1,0:T(8,128)}, f32[1,16,7168]{2,1,0:T(8,128)}, u32[]{:S(2)}, u32[]{:S(2)}) collective-permute-start(f32[1,16,7168]{2,1,0:T(8,128)} %collective-permute-done.4), channel_id=1, source_target_pairs={{0,30},{2,0},{4,2},{6,4},{8,6},{10,8},{12,10},{14,12},{16,14},{18,... | collective-permute-start | bytes 1376264 | tf_op jit(solution)/shard_map/ppermute | solution.py:96
  264.1 6.2 %collective-permute-done.5 = f32[1,16,7168]{2,1,0:T(8,128)} collective-permute-done((f32[1,16,7168]{2,1,0:T(8,128)}, f32[1,16,7168]{2,1,0:T(8,128)}, u32[]{:S(2)}, u32[]{:S(2)}) %collective-permute-start.5) | collective-permute-done | bytes 458784 | tf_op jit(solution)/shard_map/ppermute | solution.py:96
  270.4 4.6 %collective-permute-start.6 = (f32[1,16,7168]{2,1,0:T(8,128)}, f32[1,16,7168]{2,1,0:T(8,128)}, u32[]{:S(2)}, u32[]{:S(2)}) collective-permute-start(f32[1,16,7168]{2,1,0:T(8,128)} %collective-permute-done.5), channel_id=1, source_target_pairs={{0,30},{2,0},{4,2},{6,4},{8,6},{10,8},{12,10},{14,12},{16,14},{18,... | collective-permute-start | bytes 1376264 | tf_op jit(solution)/shard_map/ppermute | solution.py:96
  275.9 6.0 %collective-permute-done.6 = f32[1,16,7168]{2,1,0:T(8,128)} collective-permute-done((f32[1,16,7168]{2,1,0:T(8,128)}, f32[1,16,7168]{2,1,0:T(8,128)}, u32[]{:S(2)}, u32[]{:S(2)}) %collective-permute-start.6) | collective-permute-done | bytes 458784 | tf_op jit(solution)/shard_map/ppermute | solution.py:96
  281.9 4.6 %collective-permute-start.7 = (f32[1,16,7168]{2,1,0:T(8,128)}, f32[1,16,7168]{2,1,0:T(8,128)S(1)}, u32[]{:S(2)}, u32[]{:S(2)}) collective-permute-start(f32[1,16,7168]{2,1,0:T(8,128)} %collective-permute-done.6), channel_id=1, source_target_pairs={{0,30},{2,0},{4,2},{6,4},{8,6},{10,8},{12,10},{14,12},{16,14},{18,... | collective-permute-start | bytes 1376264 | tf_op jit(solution)/shard_map/ppermute | solution.py:96
  286.5 7.4 %collective-permute-done.7 = f32[1,16,7168]{2,1,0:T(8,128)S(1)} collective-permute-done((f32[1,16,7168]{2,1,0:T(8,128)}, f32[1,16,7168]{2,1,0:T(8,128)S(1)}, u32[]{:S(2)}, u32[]{:S(2)}) %collective-permute-start.7) | collective-permute-done | bytes 458784 | tf_op jit(solution)/shard_map/ppermute | solution.py:96
  294.7 4.5 %collective-permute-start.8 = (f32[1,16,7168]{2,1,0:T(8,128)S(1)}, f32[1,16,7168]{2,1,0:T(8,128)S(1)}, u32[]{:S(2)}, u32[]{:S(2)}) collective-permute-start(f32[1,16,7168]{2,1,0:T(8,128)S(1)} %collective-permute-done.7), channel_id=1, source_target_pairs={{0,30},{2,0},{4,2},{6,4},{8,6},{10,8},{12,10},{14,12},{16,14},{18,... | collective-permute-start | bytes 1376264 | tf_op jit(solution)/shard_map/ppermute | solution.py:96
  299.2 10.6 %collective-permute-done.8 = f32[1,16,7168]{2,1,0:T(8,128)S(1)} collective-permute-done((f32[1,16,7168]{2,1,0:T(8,128)S(1)}, f32[1,16,7168]{2,1,0:T(8,128)S(1)}, u32[]{:S(2)}, u32[]{:S(2)}) %collective-permute-start.8) | collective-permute-done | bytes 458784 | tf_op jit(solution)/shard_map/ppermute | solution.py:96
  310.6 4.7 %collective-permute-start.9 = (f32[1,16,7168]{2,1,0:T(8,128)S(1)}, f32[1,16,7168]{2,1,0:T(8,128)S(1)}, u32[]{:S(2)}, u32[]{:S(2)}) collective-permute-start(f32[1,16,7168]{2,1,0:T(8,128)S(1)} %collective-permute-done.8), channel_id=1, source_target_pairs={{0,30},{2,0},{4,2},{6,4},{8,6},{10,8},{12,10},{14,12},{16,14},{18,... | collective-permute-start | bytes 1376264 | tf_op jit(solution)/shard_map/ppermute | solution.py:96
  315.2 6.0 %collective-permute-done.9 = f32[1,16,7168]{2,1,0:T(8,128)S(1)} collective-permute-done((f32[1,16,7168]{2,1,0:T(8,128)S(1)}, f32[1,16,7168]{2,1,0:T(8,128)S(1)}, u32[]{:S(2)}, u32[]{:S(2)}) %collective-permute-start.9) | collective-permute-done | bytes 458784 | tf_op jit(solution)/shard_map/ppermute | solution.py:96
  322.0 4.6 %collective-permute-start.10 = (f32[1,16,7168]{2,1,0:T(8,128)S(1)}, f32[1,16,7168]{2,1,0:T(8,128)S(1)}, u32[]{:S(2)}, u32[]{:S(2)}) collective-permute-start(f32[1,16,7168]{2,1,0:T(8,128)S(1)} %collective-permute-done.9), channel_id=1, source_target_pairs={{0,30},{2,0},{4,2},{6,4},{8,6},{10,8},{12,10},{14,12},{16,14},{18,... | collective-permute-start | bytes 1376264 | tf_op jit(solution)/shard_map/ppermute | solution.py:96
  326.6 6.0 %collective-permute-done.10 = f32[1,16,7168]{2,1,0:T(8,128)S(1)} collective-permute-done((f32[1,16,7168]{2,1,0:T(8,128)S(1)}, f32[1,16,7168]{2,1,0:T(8,128)S(1)}, u32[]{:S(2)}, u32[]{:S(2)}) %collective-permute-start.10) | collective-permute-done | bytes 458784 | tf_op jit(solution)/shard_map/ppermute | solution.py:96
  333.4 4.6 %collective-permute-start.11 = (f32[1,16,7168]{2,1,0:T(8,128)S(1)}, f32[1,16,7168]{2,1,0:T(8,128)S(1)}, u32[]{:S(2)}, u32[]{:S(2)}) collective-permute-start(f32[1,16,7168]{2,1,0:T(8,128)S(1)} %collective-permute-done.10), channel_id=1, source_target_pairs={{0,30},{2,0},{4,2},{6,4},{8,6},{10,8},{12,10},{14,12},{16,14},{18,... | collective-permute-start | bytes 1376264 | tf_op jit(solution)/shard_map/ppermute | solution.py:96
  338.0 6.0 %collective-permute-done.11 = f32[1,16,7168]{2,1,0:T(8,128)S(1)} collective-permute-done((f32[1,16,7168]{2,1,0:T(8,128)S(1)}, f32[1,16,7168]{2,1,0:T(8,128)S(1)}, u32[]{:S(2)}, u32[]{:S(2)}) %collective-permute-start.11) | collective-permute-done | bytes 458784 | tf_op jit(solution)/shard_map/ppermute | solution.py:96
  344.0 4.6 %collective-permute-start.12 = (f32[1,16,7168]{2,1,0:T(8,128)S(1)}, f32[1,16,7168]{2,1,0:T(8,128)}, u32[]{:S(2)}, u32[]{:S(2)}) collective-permute-start(f32[1,16,7168]{2,1,0:T(8,128)S(1)} %collective-permute-done.11), channel_id=1, source_target_pairs={{0,30},{2,0},{4,2},{6,4},{8,6},{10,8},{12,10},{14,12},{16,14},{18,... | collective-permute-start | bytes 1376264 | tf_op jit(solution)/shard_map/ppermute | solution.py:96
  351.5 30.4 %all-reduce = f32[16]{0:T(128)S(1)} all-reduce(f32[16]{0:T(128)S(1)} %dynamic-update-slice), channel_id=1, replica_groups=mesh['seq'=16,'tp'=2] {'seq'}, use_global_device_ids=true, to_apply=%add | all-reduce | flops 16 | bytes 128
  388.2 4.6 %collective-permute-start.14 = (f32[1,16,7168]{2,1,0:T(8,128)}, f32[1,16,7168]{2,1,0:T(8,128)}, u32[]{:S(2)}, u32[]{:S(2)}) collective-permute-start(f32[1,16,7168]{2,1,0:T(8,128)} %collective-permute-done.13), channel_id=1, source_target_pairs={{0,30},{2,0},{4,2},{6,4},{8,6},{10,8},{12,10},{14,12},{16,14},{18,... | collective-permute-start | bytes 1376264 | tf_op jit(solution)/shard_map/ppermute | solution.py:96
  401.5 5.3 %multiply_add_fusion = f32[4,16,7168]{2,1,0:T(8,128)} fusion(f32[16,7168]{1,0:T(8,128)} %bitcast.48, f32[4]{0:T(128)S(1)} %get-tuple-element.37, f32[16,7168]{1,0:T(8,128)} %bitcast.46, f32[4]{0:T(128)S(1)} %get-tuple-element.23, f32[16,7168]{1,0:T(8,128)} %bitcast.44, f32[4]{0:T(128)S(1)} %get-tuple-element.24, f32[16,7168]{1,0:T(8,128)S(1)} %bitcast.116, ...), kind=kLoop, calls=%fused_computation.10 | loop fusion | flops 14221312 | bytes 9175296 | tf_op jit(solution)/shard_map/add | solution.py:97
  (88 shorter events, 34.6 us)
Async XLA Ops:
  7.2 191.2 %copy-start = (bf16[128,7168]{1,0:T(8,128)(2,1)S(1)}, bf16[128,7168]{1,0:T(8,128)(2,1)}, u32[]{:S(2)}) copy-start(bf16[128,7168]{1,0:T(8,128)(2,1)} %param.8) | copy-start | bytes 5505028
  7.2 56.1 %all-gather.5.cloned.1.call-start = ((), (), s32[]{:S(2)}) async-start(), calls=%async_computation.2 | async-start | bytes 4456448 | tf_op jit(solution)/shard_map/all_gather | solution.py:27
  7.9 169.6 %all-gather.7.cloned.1.call-start = ((), (), s32[]{:S(2)}) async-start(), calls=%async_computation.3 | async-start | bytes 15597568 | tf_op jit(solution)/shard_map/all_gather | solution.py:28
  10.5 59.4 %all-to-all-start = ((bf16[64,2,2048]{2,0,1:T(8,128)(2,1)}), bf16[64,2,2048]{2,0,1:T(8,128)(2,1)S(1)}, u32[]{:S(2)}, u32[]{:S(2)}) async-start(bf16[64,2,2048]{2,0,1:T(8,128)(2,1)} %bitcast.95), calls=%async_computation | async-start | bytes 1048576 | tf_op jit(solution)/shard_map/all_to_all | solution.py:46
  14.8 381.7 %all-gather.9.cloned.1.call-start = ((), (), s32[]{:S(2)}) async-start(), calls=%async_computation.4 | async-start | bytes 2228224 | tf_op jit(solution)/shard_map/all_gather | solution.py:81
  199.0 149.7 %copy-start.20 = (u32[32]{0:T(128)S(1)}, u32[32]{0:T(128)}, u32[]{:S(2)}) copy-start(u32[32]{0:T(128)} %constant.117) | copy-start | bytes 388
  199.0 150.3 %copy-start.19 = (s32[64]{0:T(128)S(1)}, s32[64]{0:T(128)}, u32[]{:S(2)}) copy-start(s32[64]{0:T(128)} %param.13) | copy-start | bytes 772
  207.8 6.0 %collective-permute-start = (f32[1,16,7168]{2,1,0:T(8,128)S(1)}, f32[1,16,7168]{2,1,0:T(8,128)S(1)}, u32[]{:S(2)}, u32[]{:S(2)}) collective-permute-start(f32[1,16,7168]{2,1,0:T(8,128)S(1)} %bitcast.105), channel_id=1, source_target_pairs={{0,30},{2,0},{4,2},{6,4},{8,6},{10,8},{12,10},{14,12},{16,14},{18,... | collective-permute-start | bytes 1376264 | tf_op jit(solution)/shard_map/ppermute | solution.py:96
  214.6 10.6 %collective-permute-start.1 = (f32[1,16,7168]{2,1,0:T(8,128)S(1)}, f32[1,16,7168]{2,1,0:T(8,128)S(1)}, u32[]{:S(2)}, u32[]{:S(2)}) collective-permute-start(f32[1,16,7168]{2,1,0:T(8,128)S(1)} %collective-permute-done), channel_id=1, source_target_pairs={{0,30},{2,0},{4,2},{6,4},{8,6},{10,8},{12,10},{14,12},{16,14},{18,... | collective-permute-start | bytes 1376264 | tf_op jit(solution)/shard_map/ppermute | solution.py:96
  226.0 10.6 %collective-permute-start.2 = (f32[1,16,7168]{2,1,0:T(8,128)S(1)}, f32[1,16,7168]{2,1,0:T(8,128)S(1)}, u32[]{:S(2)}, u32[]{:S(2)}) collective-permute-start(f32[1,16,7168]{2,1,0:T(8,128)S(1)} %collective-permute-done.1), channel_id=1, source_target_pairs={{0,30},{2,0},{4,2},{6,4},{8,6},{10,8},{12,10},{14,12},{16,14},{18,... | collective-permute-start | bytes 1376264 | tf_op jit(solution)/shard_map/ppermute | solution.py:96
  237.4 10.6 %collective-permute-start.3 = (f32[1,16,7168]{2,1,0:T(8,128)S(1)}, f32[1,16,7168]{2,1,0:T(8,128)S(1)}, u32[]{:S(2)}, u32[]{:S(2)}) collective-permute-start(f32[1,16,7168]{2,1,0:T(8,128)S(1)} %collective-permute-done.2), channel_id=1, source_target_pairs={{0,30},{2,0},{4,2},{6,4},{8,6},{10,8},{12,10},{14,12},{16,14},{18,... | collective-permute-start | bytes 1376264 | tf_op jit(solution)/shard_map/ppermute | solution.py:96
  248.7 10.6 %collective-permute-start.4 = (f32[1,16,7168]{2,1,0:T(8,128)S(1)}, f32[1,16,7168]{2,1,0:T(8,128)}, u32[]{:S(2)}, u32[]{:S(2)}) collective-permute-start(f32[1,16,7168]{2,1,0:T(8,128)S(1)} %collective-permute-done.3), channel_id=1, source_target_pairs={{0,30},{2,0},{4,2},{6,4},{8,6},{10,8},{12,10},{14,12},{16,14},{18,... | collective-permute-start | bytes 1376264 | tf_op jit(solution)/shard_map/ppermute | solution.py:96
  259.3 11.0 %collective-permute-start.5 = (f32[1,16,7168]{2,1,0:T(8,128)}, f32[1,16,7168]{2,1,0:T(8,128)}, u32[]{:S(2)}, u32[]{:S(2)}) collective-permute-start(f32[1,16,7168]{2,1,0:T(8,128)} %collective-permute-done.4), channel_id=1, source_target_pairs={{0,30},{2,0},{4,2},{6,4},{8,6},{10,8},{12,10},{14,12},{16,14},{18,... | collective-permute-start | bytes 1376264 | tf_op jit(solution)/shard_map/ppermute | solution.py:96
  270.4 11.5 %collective-permute-start.6 = (f32[1,16,7168]{2,1,0:T(8,128)}, f32[1,16,7168]{2,1,0:T(8,128)}, u32[]{:S(2)}, u32[]{:S(2)}) collective-permute-start(f32[1,16,7168]{2,1,0:T(8,128)} %collective-permute-done.5), channel_id=1, source_target_pairs={{0,30},{2,0},{4,2},{6,4},{8,6},{10,8},{12,10},{14,12},{16,14},{18,... | collective-permute-start | bytes 1376264 | tf_op jit(solution)/shard_map/ppermute | solution.py:96
  281.9 12.0 %collective-permute-start.7 = (f32[1,16,7168]{2,1,0:T(8,128)}, f32[1,16,7168]{2,1,0:T(8,128)S(1)}, u32[]{:S(2)}, u32[]{:S(2)}) collective-permute-start(f32[1,16,7168]{2,1,0:T(8,128)} %collective-permute-done.6), channel_id=1, source_target_pairs={{0,30},{2,0},{4,2},{6,4},{8,6},{10,8},{12,10},{14,12},{16,14},{18,... | collective-permute-start | bytes 1376264 | tf_op jit(solution)/shard_map/ppermute | solution.py:96
  294.7 15.1 %collective-permute-start.8 = (f32[1,16,7168]{2,1,0:T(8,128)S(1)}, f32[1,16,7168]{2,1,0:T(8,128)S(1)}, u32[]{:S(2)}, u32[]{:S(2)}) collective-permute-start(f32[1,16,7168]{2,1,0:T(8,128)S(1)} %collective-permute-done.7), channel_id=1, source_target_pairs={{0,30},{2,0},{4,2},{6,4},{8,6},{10,8},{12,10},{14,12},{16,14},{18,... | collective-permute-start | bytes 1376264 | tf_op jit(solution)/shard_map/ppermute | solution.py:96
  310.6 10.7 %collective-permute-start.9 = (f32[1,16,7168]{2,1,0:T(8,128)S(1)}, f32[1,16,7168]{2,1,0:T(8,128)S(1)}, u32[]{:S(2)}, u32[]{:S(2)}) collective-permute-start(f32[1,16,7168]{2,1,0:T(8,128)S(1)} %collective-permute-done.8), channel_id=1, source_target_pairs={{0,30},{2,0},{4,2},{6,4},{8,6},{10,8},{12,10},{14,12},{16,14},{18,... | collective-permute-start | bytes 1376264 | tf_op jit(solution)/shard_map/ppermute | solution.py:96
  322.0 10.6 %collective-permute-start.10 = (f32[1,16,7168]{2,1,0:T(8,128)S(1)}, f32[1,16,7168]{2,1,0:T(8,128)S(1)}, u32[]{:S(2)}, u32[]{:S(2)}) collective-permute-start(f32[1,16,7168]{2,1,0:T(8,128)S(1)} %collective-permute-done.9), channel_id=1, source_target_pairs={{0,30},{2,0},{4,2},{6,4},{8,6},{10,8},{12,10},{14,12},{16,14},{18,... | collective-permute-start | bytes 1376264 | tf_op jit(solution)/shard_map/ppermute | solution.py:96
  333.4 10.6 %collective-permute-start.11 = (f32[1,16,7168]{2,1,0:T(8,128)S(1)}, f32[1,16,7168]{2,1,0:T(8,128)S(1)}, u32[]{:S(2)}, u32[]{:S(2)}) collective-permute-start(f32[1,16,7168]{2,1,0:T(8,128)S(1)} %collective-permute-done.10), channel_id=1, source_target_pairs={{0,30},{2,0},{4,2},{6,4},{8,6},{10,8},{12,10},{14,12},{16,14},{18,... | collective-permute-start | bytes 1376264 | tf_op jit(solution)/shard_map/ppermute | solution.py:96
  344.0 39.3 %copy-start.17 = (f32[1,16,7168]{2,1,0:T(8,128)}, f32[1,16,7168]{2,1,0:T(8,128)S(1)}, u32[]{:S(2)}) copy-start(f32[1,16,7168]{2,1,0:T(8,128)S(1)} %collective-permute-done.11) | copy-start | bytes 1376260
  344.0 37.9 %collective-permute-start.12 = (f32[1,16,7168]{2,1,0:T(8,128)S(1)}, f32[1,16,7168]{2,1,0:T(8,128)}, u32[]{:S(2)}, u32[]{:S(2)}) collective-permute-start(f32[1,16,7168]{2,1,0:T(8,128)S(1)} %collective-permute-done.11), channel_id=1, source_target_pairs={{0,30},{2,0},{4,2},{6,4},{8,6},{10,8},{12,10},{14,12},{16,14},{18,... | collective-permute-start | bytes 1376264 | tf_op jit(solution)/shard_map/ppermute | solution.py:96
  381.9 6.4 %collective-permute-start.13 = (f32[1,16,7168]{2,1,0:T(8,128)}, f32[1,16,7168]{2,1,0:T(8,128)}, u32[]{:S(2)}, u32[]{:S(2)}) collective-permute-start(f32[1,16,7168]{2,1,0:T(8,128)} %collective-permute-done.12), channel_id=1, source_target_pairs={{0,30},{2,0},{4,2},{6,4},{8,6},{10,8},{12,10},{14,12},{16,14},{18,... | collective-permute-start | bytes 1376264 | tf_op jit(solution)/shard_map/ppermute | solution.py:96
  383.3 12.4 %all-to-all-start.1 = ((bf16[2,64,2048]{2,1,0:T(8,128)(2,1)}), bf16[2,64,2048]{2,1,0:T(8,128)(2,1)S(1)}, u32[]{:S(2)}, u32[]{:S(2)}) async-start(bf16[2,64,2048]{2,1,0:T(8,128)(2,1)} %bitcast.10), calls=%async_computation.1 | async-start | bytes 1048576 | tf_op jit(solution)/shard_map/all_to_all | solution.py:63
  388.2 13.2 %collective-permute-start.14 = (f32[1,16,7168]{2,1,0:T(8,128)}, f32[1,16,7168]{2,1,0:T(8,128)}, u32[]{:S(2)}, u32[]{:S(2)}) collective-permute-start(f32[1,16,7168]{2,1,0:T(8,128)} %collective-permute-done.13), channel_id=1, source_target_pairs={{0,30},{2,0},{4,2},{6,4},{8,6},{10,8},{12,10},{14,12},{16,14},{18,... | collective-permute-start | bytes 1376264 | tf_op jit(solution)/shard_map/ppermute | solution.py:96
  395.7 5.7 %copy-start.18 = (f32[1,16,7168]{2,1,0:T(8,128)S(1)}, f32[1,16,7168]{2,1,0:T(8,128)}, u32[]{:S(2)}) copy-start(f32[1,16,7168]{2,1,0:T(8,128)} %copy-done.17) | copy-start | bytes 1376260
  396.6 4.9 %copy-start.4 = (f32[1,16,7168]{2,1,0:T(8,128)S(1)}, f32[1,16,7168]{2,1,0:T(8,128)}, u32[]{:S(2)}) copy-start(f32[1,16,7168]{2,1,0:T(8,128)} %copy-done.3) | copy-start | bytes 1376260
  396.6 4.9 %copy-start.6 = (f32[1,16,7168]{2,1,0:T(8,128)S(1)}, f32[1,16,7168]{2,1,0:T(8,128)}, u32[]{:S(2)}) copy-start(f32[1,16,7168]{2,1,0:T(8,128)} %copy-done.5) | copy-start | bytes 1376260
  396.6 4.9 %copy-start.8 = (f32[1,16,7168]{2,1,0:T(8,128)S(1)}, f32[1,16,7168]{2,1,0:T(8,128)}, u32[]{:S(2)}) copy-start(f32[1,16,7168]{2,1,0:T(8,128)} %copy-done.7) | copy-start | bytes 1376260
  396.6 4.9 %copy-start.10 = (f32[1,16,7168]{2,1,0:T(8,128)S(1)}, f32[1,16,7168]{2,1,0:T(8,128)}, u32[]{:S(2)}) copy-start(f32[1,16,7168]{2,1,0:T(8,128)} %copy-done.9) | copy-start | bytes 1376260
  396.6 4.9 %copy-start.12 = (f32[1,16,7168]{2,1,0:T(8,128)S(1)}, f32[1,16,7168]{2,1,0:T(8,128)}, u32[]{:S(2)}) copy-start(f32[1,16,7168]{2,1,0:T(8,128)} %copy-done.11) | copy-start | bytes 1376260
  396.6 4.9 %copy-start.14 = (f32[1,16,7168]{2,1,0:T(8,128)S(1)}, f32[1,16,7168]{2,1,0:T(8,128)}, u32[]{:S(2)}) copy-start(f32[1,16,7168]{2,1,0:T(8,128)} %copy-done.13) | copy-start | bytes 1376260
  396.6 4.9 %copy-start.16 = (f32[1,16,7168]{2,1,0:T(8,128)S(1)}, f32[1,16,7168]{2,1,0:T(8,128)}, u32[]{:S(2)}) copy-start(f32[1,16,7168]{2,1,0:T(8,128)} %copy-done.15) | copy-start | bytes 1376260
  (9 other events, 11.2 us)
Sparse Core Ops, SparseCore 0:
  10.1 53.0 all-gather.4
  65.6 111.8 all-gather.6
  276.0 42.7 all-gather.8
